TPU v7x, 256 devices: a whole 4x4x8 slice. The times are simulated.
256 devices in a mesh: dp: 4 (over x), expert: 64 (over y, z, core).
Axes of the slice: x: 4, y: 4, z: 8, core: 2. Of those that a mesh axis runs over, the one named last changes fastest.
Arguments:
- tokens: bfloat16 [8192, 4096], P('expert', 'dp'), may hold values from -6 to 6
- routes: int32 [8192, 4], P('expert'), may hold values from 0 to 63, all different within a row; in each aligned block of 128 rows (0 to 127, 128 to 255, ...) at most 16 rows name the same one
- route_weights: float32 [8192, 4], P('expert'), may hold values from 0.1 to 1
- gate_weight: bfloat16 [64, 4096, 1536], P('expert', None, 'dp'), may hold values from -0.09375 to 0.09375
- up_weight: bfloat16 [64, 4096, 1536], P('expert', None, 'dp'), may hold values from -0.09375 to 0.09375
- down_weight: bfloat16 [64, 1536, 4096], P('expert', 'dp'), may hold values from -0.15625 to 0.15625
- sketch_basis: bfloat16 [1536, 128], P('dp'), may hold values from -0.15625 to 0.15625
Outputs:
- mixed: bfloat16 [8192, 4096], P('expert', 'dp')
- sketch: float32 [64, 128, 1536], P('expert', None, 'dp')
Inputs may be any that keep to these rules, and one draw needn't show every extreme that they name: `routes`: each row names 4 different experts; within the rows of one device no expert is named more than 16 times, a bound that some block reaches.
All inputs are finite; a program needn't handle non-finite values.
Results may differ from a plain program's by a relative error of at most 0.017.
Values may be sent and summed in bfloat16 or wider, within the bound.
No kernel may reach another device: no remote copies, remote signals or barrier semaphores. Data moves between devices by JAX's collectives and lax.ppermute only.
A program may use at most 128 MiB of HBM per device.

v0:
```python
import jax
import jax.numpy as jnp
from jax import lax
from jax.sharding import PartitionSpec as P

ridge_term = 1.0


def gram_matrix(factor_rows):
    return jnp.dot(factor_rows.T, factor_rows, precision=lax.Precision.HIGHEST)


def body(tokens, routes, route_weights, gate_weight, up_weight, down_weight, sketch_basis):
    owners = lax.axis_size("expert")
    token_count, route_count = routes.shape
    pair_count = token_count * route_count
    capacity = 2 * pair_count // owners
    slot_total = owners * capacity
    route_list = routes.reshape(-1)
    onehot = (route_list[:, None] == jnp.arange(owners, dtype=jnp.int32)[None, :]).astype(jnp.int32)
    before = jnp.cumsum(onehot, axis=0) - onehot
    slot_of = jnp.sum(before * onehot, axis=1)
    counts = jnp.sum(onehot, axis=0)
    target = route_list * capacity + slot_of
    source_pair = (
        jnp.zeros((slot_total,), jnp.int32).at[target].set(jnp.arange(pair_count, dtype=jnp.int32))
    )
    source_token = source_pair // route_count
    count_wire = counts.astype(jnp.bfloat16)
    features = lax.all_gather(tokens, "dp", axis=1, tiled=True)
    outgoing = features[source_token].reshape(owners, capacity, features.shape[1])
    arrived, arrived_counts = (
        lax.all_to_all(outgoing, "expert", split_axis=0, concat_axis=0, tiled=True),
        lax.all_to_all(count_wire, "expert", split_axis=0, concat_axis=0, tiled=True),
    )
    width = arrived.shape[2]
    live_count = arrived_counts.astype(jnp.int32)
    live_mask = (jnp.arange(capacity, dtype=jnp.int32)[None, :] < live_count[:, None]).reshape(-1)
    slot_rows = jnp.where(
        live_mask[:, None], arrived.reshape(slot_total, width), jnp.zeros((), jnp.bfloat16)
    )
    gate_local = gate_weight[0]
    up_local = up_weight[0]
    down_local = down_weight[0]
    gate_val = jnp.dot(slot_rows, gate_local, preferred_element_type=jnp.float32)
    up_val = jnp.dot(slot_rows, up_local, preferred_element_type=jnp.float32)
    hidden_block = (jax.nn.silu(gate_val) * up_val).astype(jnp.bfloat16)
    partial_value = jnp.dot(hidden_block, down_local, preferred_element_type=jnp.float32)
    sums = lax.psum_scatter(
        partial_value.reshape(owners, capacity, width).astype(jnp.bfloat16),
        "dp",
        scatter_dimension=2,
        tiled=True,
    )
    returned = lax.all_to_all(sums, "expert", split_axis=0, concat_axis=0, tiled=True)
    picked = returned.reshape(slot_total, returned.shape[2])[target]
    weighted = jnp.einsum(
        "tkd,tk->td",
        picked.reshape(token_count, route_count, returned.shape[2]).astype(jnp.float32),
        route_weights,
    )
    mixed = weighted.astype(jnp.bfloat16)
    sketch_part = jnp.dot(hidden_block, sketch_basis, preferred_element_type=jnp.float32)
    sketch_width = sketch_part.shape[1]
    eye_matrix = jnp.eye(sketch_width, dtype=jnp.float32)
    sketch_full = lax.psum(sketch_part.astype(jnp.bfloat16), "dp").astype(jnp.float32)
    lower_factor = jnp.linalg.cholesky(gram_matrix(sketch_full) + ridge_term * eye_matrix)
    projected = jnp.dot(
        sketch_full.T, hidden_block.astype(jnp.float32), precision=lax.Precision.HIGHEST
    )
    whitened = jax.scipy.linalg.solve_triangular(lower_factor, projected, lower=True)
    return (mixed, whitened[None])


def solution(mesh):
    return jax.shard_map(
        body,
        mesh=mesh,
        in_specs=(
            P("expert", "dp"),
            P("expert", None),
            P("expert", None),
            P("expert", None, "dp"),
            P("expert", None, "dp"),
            P("expert", "dp", None),
            P("dp", None),
        ),
        out_specs=(P("expert", "dp"), P("expert", None, "dp")),
        check_vma=False,
    )
```

profile of v0, /device:TPU:8, one launch (start us, length us, event | category | flops | bytes accessed | tf_op | source)
XLA Modules:
  0.0 463.0 jit_solution(337429624355263726)
XLA Ops:
  7.2 0.0 copy-start
  7.2 0.0 all-gather.2.cloned.1.call-start
  7.2 0.7 all-gather.2.cloned.1.call-update
  7.9 1.0 copy.21
  8.9 0.1 eq.33
  9.0 0.1 eq.29
  9.1 1.2 reduce-window.6
  10.3 0.2 slice_reduce_fusion
  10.6 0.2 convert_reduce_fusion
  10.8 0.7 copy.22
  11.5 12.1 %all-to-all-start = ((bf16[64,1,1]{2,1,0:T(2,128)(2,1)}), bf16[64,1,1]{2,1,0:T(2,128)(2,1)S(1)}, u32[]{:S(2)}, u32[]{:S(2)}) async-start(bf16[64,1,1]{2,1,0:T(2,128)(2,1)} %copy.22), calls=%async_computation | async-start | bytes 65536 | tf_op jit(solution)/shard_map/all_to_all | solution.py:34
  23.6 0.7 broadcast_multiply_fusion
  24.3 0.1 copy.23
  24.5 0.1 mul.28
  24.6 2.4 scatter_custom_fusion
  27.1 12.2 %all-gather.2.cloned.1.call-done = bf16[128,4096]{1,0:T(8,128)(2,1)} async-done(((bf16[128,1024]{1,0:T(8,128)(2,1)}), bf16[128,4096]{1,0:T(8,128)(2,1)}) %all-gather.2.cloned.1.call-update) | async-done | bytes 1048592 | tf_op jit(solution)/shard_map/all_gather | solution.py:30
  39.2 16.4 %gather_fusion = bf16[1024,4096]{1,0:T(8,128)(2,1)} fusion(bf16[128,4096]{1,0:T(8,128)(2,1)} %all-gather.2.cloned.1.call-done, s32[1024]{0:T(1024)S(1)} %fusion.15), kind=kCustom, calls=%fused_computation | custom fusion | bytes 16781312 | tf_op jit(solution)/shard_map/gather | solution.py:31
  55.7 0.0 all-to-all-done
  55.7 10.8 %all-to-all-start.1 = ((bf16[64,16,4096]{2,1,0:T(8,128)(2,1)}), bf16[64,16,4096]{2,1,0:T(8,128)(2,1)}, u32[]{:S(2)}, u32[]{:S(2)}) async-start(bf16[64,16,4096]{2,1,0:T(8,128)(2,1)} %bitcast.60), calls=%async_computation.1 | async-start | bytes 16777216 | tf_op jit(solution)/shard_map/all_to_all | solution.py:33
  66.4 0.2 reduce-scatter.2.cloned.1.call-start
  66.7 1.2 convert_reduce_fusion.1
  67.9 0.1 iota_compare_fusion.5
  68.0 182.8 %all-to-all-done.1 = bf16[64,16,4096]{2,1,0:T(8,128)(2,1)} async-done(((bf16[64,16,4096]{2,1,0:T(8,128)(2,1)}), bf16[64,16,4096]{2,1,0:T(8,128)(2,1)}, u32[]{:S(2)}, u32[]{:S(2)}) %all-to-all-start.1) | async-done | bytes 8388640 | tf_op jit(solution)/shard_map/all_to_all | solution.py:33
  250.8 7.2 %broadcast_select_fusion = bf16[64,16,4096]{2,1,0:T(8,128)(2,1)} fusion(bf16[64,16,4096]{2,1,0:T(8,128)(2,1)} %all-to-all-done.1, pred[64,16]{1,0:T(8,128)(4,1)S(1)} %iota_compare_fusion.5), kind=kLoop, calls=%fused_computation.3 | loop fusion | flops 4194304 | bytes 16778240 | tf_op jit(solution)/shard_map/jit(_where)/select_n | solution.py:39
  258.0 0.0 copy-start.1
  258.0 0.0 copy-start.5
  258.0 8.0 %fusion.3 = f32[1024,384]{1,0:T(8,128)S(1)} fusion(bf16[1024,4096]{1,0:T(8,128)(2,1)} %bitcast.61, bf16[1,4096,384]{2,1,0:T(8,128)(2,1)} %param.10), kind=kOutput, calls=%fused_computation.8 | convolution fusion | flops 3221225472 | bytes 13107200 | tf_op jit(solution)/shard_map/dot_general | solution.py:45
  266.0 0.0 copy-done.1
  266.0 0.0 copy-done.5
  266.0 4.6 multiply_convert_fusion
  270.6 0.0 copy-start.2
  270.6 0.9 copy-done.2
  271.5 0.0 copy-done
  271.5 6.6 %convolution_convert_fusion = bf16[64,16,4096]{2,1,0:T(8,128)(2,1)} fusion(bf16[64,16,384]{2,1,0:T(8,128)(2,1)S(1)} %bitcast.63, bf16[1,384,4096]{2,1,0:T(8,128)(2,1)S(1)} %copy-done), kind=kOutput, calls=%fused_computation.4 | convolution fusion | flops 3225419776 | bytes 12320768 | tf_op jit(solution)/shard_map/dot_general | solution.py:48
  278.1 0.0 reduce-scatter.2.cloned.1.call-update
  278.1 0.0 copy-start.3
  278.2 0.0 copy-start.4
  278.2 80.3 %reduce-scatter.2.cloned.1.call-done = bf16[64,16,1024]{2,1,0:T(8,128)(2,1)} async-done(((bf16[64,16,4096]{2,1,0:T(8,128)(2,1)}), bf16[64,16,1024]{2,1,0:T(8,128)(2,1)}) %reduce-scatter.2.cloned.1.call-update) | async-done | bytes 2097168 | tf_op jit(solution)/shard_map/reduce_scatter | solution.py:49
  358.5 10.8 %all-to-all-start.2 = ((bf16[64,16,1024]{2,1,0:T(8,128)(2,1)}), bf16[64,16,1024]{2,1,0:T(8,128)(2,1)}, u32[]{:S(2)}, u32[]{:S(2)}) async-start(bf16[64,16,1024]{2,1,0:T(8,128)(2,1)} %reduce-scatter.2.cloned.1.call-done), calls=%async_computation.3 | async-start | bytes 4194304 | tf_op jit(solution)/shard_map/all_to_all | solution.py:55
  369.2 0.3 all-reduce.2.cloned.1.call-start
  369.5 0.0 copy-done.3
  369.5 2.2 convolution_convert_fusion.1
  371.7 0.0 all-reduce.2.cloned.1.call-update
  371.7 0.0 copy-done.4
  371.7 0.2 copy.27
  371.9 47.3 %all-reduce.2.cloned.1.call-done = bf16[1024,128]{1,0:T(8,128)(2,1)} async-done(((bf16[1024,128]{1,0:T(8,128)(2,1)}), bf16[1024,128]{1,0:T(8,128)(2,1)}) %all-reduce.2.cloned.1.call-update) | async-done | bytes 262160 | tf_op jit(solution)/shard_map/psum | solution.py:66
  419.2 1.3 fusion.20
  420.5 0.1 copy.26
  420.7 11.7 %cholesky.17 = f32[128,128]{1,0:T(8,128)S(1)} custom-call(f32[128,128]{1,0:T(8,128)S(1)} %fusion.13), custom_call_target="Cholesky" | custom-call | tf_op jit(solution)/shard_map/jit(cholesky)/cholesky | solution.py:67
  432.4 0.6 compare_reduce_fusion
  433.1 0.7 fusion.10
  433.7 9.8 %custom-call.7 = f32[1,128,128]{1,2,0:T(8,128)S(1)} custom-call(f32[1,128,128]{2,1,0:T(8,128)S(1)} %fusion.10), custom_call_target="InvertDiagBlocksLowerTriangular" | custom-call | tf_op jit(solution)/shard_map/jit(_solve_triangular)/triangular_solve | solution.py:71
  443.5 1.5 fusion.21
  445.1 1.0 convolution_bitcast_fusion
  446.1 0.0 all-to-all-done.2
  446.1 5.3 %gather_fusion.1 = bf16[512,1024]{1,0:T(8,128)(2,1)} fusion(bf16[1024,1024]{1,0:T(8,128)(2,1)} %bitcast.11, s32[1024]{0:T(1024)S(1)} %pad_clamp_fusion), kind=kCustom, calls=%fused_computation.1 | custom fusion | bytes 2099200 | tf_op jit(solution)/shard_map/gather | solution.py:56
  451.5 2.3 reshape.115
  453.7 1.9 fusion.19
  455.7 0.8 copy.32
  (10 shorter events, 0.2 us)
Async XLA Ops:
  7.2 264.3 %copy-start = (bf16[1,384,4096]{2,1,0:T(8,128)(2,1)S(1)}, bf16[1,384,4096]{2,1,0:T(8,128)(2,1)}, u32[]{:S(2)}) copy-start(bf16[1,384,4096]{2,1,0:T(8,128)(2,1)} %param.12) | copy-start | bytes 9437188
  7.2 32.0 %all-gather.2.cloned.1.call-start = ((), (), s32[]{:S(2)}) async-start(), calls=%async_computation.4 | async-start | bytes 1310720 | tf_op jit(solution)/shard_map/all_gather | solution.py:30
  11.5 44.1 %all-to-all-start = ((bf16[64,1,1]{2,1,0:T(2,128)(2,1)}), bf16[64,1,1]{2,1,0:T(2,128)(2,1)S(1)}, u32[]{:S(2)}, u32[]{:S(2)}) async-start(bf16[64,1,1]{2,1,0:T(2,128)(2,1)} %copy.22), calls=%async_computation | async-start | bytes 65536 | tf_op jit(solution)/shard_map/all_to_all | solution.py:34
  55.7 195.1 %all-to-all-start.1 = ((bf16[64,16,4096]{2,1,0:T(8,128)(2,1)}), bf16[64,16,4096]{2,1,0:T(8,128)(2,1)}, u32[]{:S(2)}, u32[]{:S(2)}) async-start(bf16[64,16,4096]{2,1,0:T(8,128)(2,1)} %bitcast.60), calls=%async_computation.1 | async-start | bytes 16777216 | tf_op jit(solution)/shard_map/all_to_all | solution.py:33
  66.4 292.0 %reduce-scatter.2.cloned.1.call-start = ((), (), s32[]{:S(2)}) async-start(), calls=%async_computation.5 | async-start | bytes 10485760 | tf_op jit(solution)/shard_map/reduce_scatter | solution.py:49
  258.0 8.0 %copy-start.1 = (bf16[64,16,4096]{2,1,0:T(8,128)(2,1)S(1)}, bf16[64,16,4096]{2,1,0:T(8,128)(2,1)}, u32[]{:S(2)}) copy-start(bf16[64,16,4096]{2,1,0:T(8,128)(2,1)} %broadcast_select_fusion) | copy-start | bytes 25165828
  258.0 8.0 %copy-start.5 = (bf16[1,4096,384]{2,1,0:T(8,128)(2,1)S(1)}, bf16[1,4096,384]{2,1,0:T(8,128)(2,1)}, u32[]{:S(2)}) copy-start(bf16[1,4096,384]{2,1,0:T(8,128)(2,1)} %param.11) | copy-start | bytes 9437188
  270.6 0.9 copy-start.2
  278.1 91.4 %copy-start.3 = (bf16[384,128]{1,0:T(8,128)(2,1)S(1)}, bf16[384,128]{1,0:T(8,128)(2,1)}, u32[]{:S(2)}) copy-start(bf16[384,128]{1,0:T(8,128)(2,1)} %param.13) | copy-start | bytes 294916
  278.2 93.6 %copy-start.4 = (f32[128,4]{0,1:T(4,128)S(1)}, f32[128,4]{0,1:T(4,128)}, u32[]{:S(2)}) copy-start(f32[128,4]{0,1:T(4,128)} %param.9) | copy-start | bytes 6148
  358.5 87.7 %all-to-all-start.2 = ((bf16[64,16,1024]{2,1,0:T(8,128)(2,1)}), bf16[64,16,1024]{2,1,0:T(8,128)(2,1)}, u32[]{:S(2)}, u32[]{:S(2)}) async-start(bf16[64,16,1024]{2,1,0:T(8,128)(2,1)} %reduce-scatter.2.cloned.1.call-done), calls=%async_computation.3 | async-start | bytes 4194304 | tf_op jit(solution)/shard_map/all_to_all | solution.py:55
  369.2 50.0 %all-reduce.2.cloned.1.call-start = ((), (), s32[]{:S(2)}) async-start(), calls=%async_computation.6 | async-start | bytes 524288 | tf_op jit(solution)/shard_map/psum | solution.py:66
Sparse Core Ops, SparseCore 0:
  9.8 29.3 all-gather.1
  278.3 80.1 reduce-scatter.1
  373.0 46.2 all-reduce.1
where the time goes:
time: 464 us; the launch traced here: 463 us
  waiting for transfers between devices  323 us (70%)
  starting transfers between devices  34.1 us (7%)
  other arithmetic  33.6 us (7%)
  local copies, waits for them, and re-layouts  30.8 us (7%)
  matrix products  27.2 us (6%)
  between operations  14 us (3%)
    all_to_all x1, waiting for transfers between devices, body(): lax.all_to_all(outgoing, 'expert', split_axis=0, concat_axis=0, tiled=True)  183 us
    reduce_scatter x1, waiting for transfers between devices, body(): lax.psum_scatter(partial_value.reshape(owners, capacity, width).astype(jn...  80.3 us
    psum x1, waiting for transfers between devices, body(): lax.psum(sketch_part.astype(jnp.bfloat16), 'dp').astype(jnp.float32)  47.3 us
    gather x1, local copies, waits for them, and re-layouts, body(): features[source_token].reshape(owners, capacity, features.shape[1])  16.4 us
    another operation x3, other arithmetic, body(): jnp.linalg.cholesky(gram_matrix(sketch_full) + ridge_term * eye_matrix)  12.4 us
    all_gather x1, waiting for transfers between devices, body(): features = lax.all_gather(tokens, 'dp', axis=1, tiled=True)  12.2 us
    all_to_all x1, starting transfers between devices, body(): lax.all_to_all(count_wire, 'expert', split_axis=0, concat_axis=0, tiled=T...  12.1 us
    all_to_all x1, starting transfers between devices, body(): lax.all_to_all(sums, 'expert', split_axis=0, concat_axis=0, tiled=True)  10.8 us
  transfers between devices with their start and end apart: 6, of which 4 were waited for; matrix products, arithmetic and copies ran while one was open for 12% of the time, Pallas kernels for 0%

commit v1 on v0

--- a/solution.py
+++ b/solution.py
@@ -1,9 +1,34 @@
+import functools
 import jax
 import jax.numpy as jnp
 from jax import lax
 from jax.sharding import PartitionSpec as P
+from jax.lax import axis_index, axis_size, ppermute
 
 ridge_term = 1.0
+
+
+def remake_quotas_for(packet, which_axis, in_dim):
+    shares = axis_size(which_axis)
+    ledger = []
+    for tick in range(shares):
+        ledger.append((tick, (tick + 1) % shares))
+    trail = []
+    for tick in range(shares):
+        trail.append((tick, (tick - 1) % shares))
+    y, big = ([packet], [packet])
+    for _ in range(shares // 2):
+        y.append(ppermute(y[-1], axis_name=which_axis, perm=ledger))
+    for _ in range((shares - 1) // 2):
+        big.append(ppermute(big[-1], which_axis, perm=trail))
+    return jnp.roll(
+        jnp.concatenate([*y[::-1], *big[1:]], axis=in_dim),
+        (axis_index(which_axis) - shares // 2) * packet.shape[in_dim],
+        axis=in_dim,
+    )
+
+
+_prepare_entries = functools.partial(remake_quotas_for, which_axis="dp", in_dim=1)
 
 
 def gram_matrix(factor_rows):
@@ -27,7 +52,7 @@
     )
     source_token = source_pair // route_count
     count_wire = counts.astype(jnp.bfloat16)
-    features = lax.all_gather(tokens, "dp", axis=1, tiled=True)
+    features = _prepare_entries(tokens)
     outgoing = features[source_token].reshape(owners, capacity, features.shape[1])
     arrived, arrived_counts = (
         lax.all_to_all(outgoing, "expert", split_axis=0, concat_axis=0, tiled=True),

time: 464 us -> 469 us (1.011)
  waiting for transfers between devices: 323 us -> 316 us
  local copies, waits for them, and re-layouts: 30.8 us -> 37.6 us
    all_gather x1 -> x0, waiting for transfers between devices: 12.2 us -> none  [body(): features = lax.all_gather(tokens, 'dp', axis=1, tiled=True)]
    ppermute x0 -> x3, waiting for transfers between devices: none -> 7.13 us  [the longest x2 7.12 us: remake_quotas_for(): y.append(ppermute(y[-1], axis_name=which_axis, perm=ledger))]
  transfers between devices with their start and end apart: 6 -> 8, of which waited for: 4 -> 4; matrix products, arithmetic and copies ran while one was open for 12% -> 13% of each run, Pallas kernels for 0% -> 0%
where the time goes in v1:
time: 469 us; the launch traced here: 468 us
  waiting for transfers between devices  316 us (67%)
  local copies, waits for them, and re-layouts  37.6 us (8%)
  starting transfers between devices  37.5 us (8%)
  other arithmetic  35.4 us (8%)
  matrix products  27.2 us (6%)
  between operations  14.3 us (3%)
    all_to_all x1, waiting for transfers between devices, body(): lax.all_to_all(outgoing, 'expert', split_axis=0, concat_axis=0, tiled=True)  183 us
    reduce_scatter x1, waiting for transfers between devices, body(): lax.psum_scatter(partial_value.reshape(owners, capacity, width).astype(jn...  78.8 us
    psum x1, waiting for transfers between devices, body(): lax.psum(sketch_part.astype(jnp.bfloat16), 'dp').astype(jnp.float32)  47.4 us
    gather x1, local copies, waits for them, and re-layouts, body(): features[source_token].reshape(owners, capacity, features.shape[1])  16.4 us
    another operation x3, other arithmetic, body(): jnp.linalg.cholesky(gram_matrix(sketch_full) + ridge_term * eye_matrix)  12.4 us
    all_to_all x1, starting transfers between devices, body(): lax.all_to_all(count_wire, 'expert', split_axis=0, concat_axis=0, tiled=T...  12.1 us
    all_to_all x1, starting transfers between devices, body(): lax.all_to_all(sums, 'expert', split_axis=0, concat_axis=0, tiled=True)  10.8 us
    all_to_all x1, starting transfers between devices, body(): lax.all_to_all(outgoing, 'expert', split_axis=0, concat_axis=0, tiled=True)  10.5 us
  transfers between devices with their start and end apart: 8, of which 4 were waited for; matrix products, arithmetic and copies ran while one was open for 13% of the time, Pallas kernels for 0%

profile of v1, /device:TPU:8, one launch (start us, length us, event | category | flops | bytes accessed | tf_op | source)
XLA Modules:
  0.0 468.1 jit_solution(14223786993040600681)
XLA Ops:
  7.2 0.0 copy-start
  7.2 0.0 copy-start.3
  7.2 1.6 collective-permute-start
  8.8 1.7 collective-permute-start.2
  10.5 0.8 copy.21
  11.3 0.1 eq.36
  11.4 0.1 eq.32
  11.5 0.7 fusion.9
  12.2 2.4 reduce-window.6
  14.6 0.2 slice_reduce_fusion
  14.8 0.2 convert_reduce_fusion
  15.0 0.7 copy.22
  15.8 12.1 %all-to-all-start = ((bf16[64,1,1]{2,1,0:T(2,128)(2,1)}), bf16[64,1,1]{2,1,0:T(2,128)(2,1)S(1)}, u32[]{:S(2)}, u32[]{:S(2)}) async-start(bf16[64,1,1]{2,1,0:T(2,128)(2,1)} %copy.22), calls=%async_computation | async-start | bytes 65536 | tf_op jit(solution)/shard_map/all_to_all | solution.py:59
  27.9 0.7 broadcast_multiply_fusion
  28.6 0.1 copy.23
  28.7 0.1 mul.32
  28.8 0.0 collective-permute-done
  28.8 0.4 collective-permute-start.1
  29.2 2.4 scatter_custom_fusion
  31.6 7.1 %collective-permute-done.1 = bf16[128,1024]{1,0:T(8,128)(2,1)} collective-permute-done((bf16[128,1024]{1,0:T(8,128)(2,1)}, bf16[128,1024]{1,0:T(8,128)(2,1)}, u32[]{:S(2)}, u32[]{:S(2)}) %collective-permute-start.1) | collective-permute-done | bytes 262176 | tf_op jit(solution)/shard_map/ppermute | solution.py:21
  38.8 1.0 constant_dynamic-update-slice_fusion.7
  39.7 1.0 constant_dynamic-update-slice_fusion.6
  40.7 0.0 copy-done.3
  40.7 0.0 collective-permute-done.2
  40.8 1.0 constant_dynamic-update-slice_fusion.4
  41.7 1.0 constant_dynamic-update-slice_fusion.3
  42.7 1.0 constant_dynamic-update-slice_fusion.2
  43.7 1.0 constant_dynamic-update-slice_fusion
  44.7 1.1 constant_dynamic-slice_fusion
  45.7 16.4 %gather_fusion = bf16[1024,4096]{1,0:T(8,128)(2,1)} fusion(bf16[128,4096]{1,0:T(8,128)(2,1)} %constant_dynamic-slice_fusion, s32[1024]{0:T(1024)S(1)} %fusion.15), kind=kCustom, calls=%fused_computation | custom fusion | bytes 16781312 | tf_op jit(solution)/shard_map/gather | solution.py:56
  62.2 0.0 all-to-all-done
  62.2 10.5 %all-to-all-start.1 = ((bf16[64,16,4096]{2,1,0:T(8,128)(2,1)}), bf16[64,16,4096]{2,1,0:T(8,128)(2,1)}, u32[]{:S(2)}, u32[]{:S(2)}) async-start(bf16[64,16,4096]{2,1,0:T(8,128)(2,1)} %bitcast.60), calls=%async_computation.1 | async-start | bytes 16777216 | tf_op jit(solution)/shard_map/all_to_all | solution.py:58
  72.7 0.2 reduce-scatter.2.cloned.1.call-start
  72.9 1.2 convert_reduce_fusion.1
  74.2 0.1 iota_compare_fusion.5
  74.2 182.8 %all-to-all-done.1 = bf16[64,16,4096]{2,1,0:T(8,128)(2,1)} async-done(((bf16[64,16,4096]{2,1,0:T(8,128)(2,1)}), bf16[64,16,4096]{2,1,0:T(8,128)(2,1)}, u32[]{:S(2)}, u32[]{:S(2)}) %all-to-all-start.1) | async-done | bytes 8388640 | tf_op jit(solution)/shard_map/all_to_all | solution.py:58
  257.1 7.2 %broadcast_select_fusion = bf16[64,16,4096]{2,1,0:T(8,128)(2,1)} fusion(bf16[64,16,4096]{2,1,0:T(8,128)(2,1)} %all-to-all-done.1, pred[64,16]{1,0:T(8,128)(4,1)S(1)} %iota_compare_fusion.5), kind=kLoop, calls=%fused_computation.3 | loop fusion | flops 4194304 | bytes 16778240 | tf_op jit(solution)/shard_map/jit(_where)/select_n | solution.py:64
  264.3 8.0 %fusion.3 = f32[1024,384]{1,0:T(8,128)S(1)} fusion(bf16[1024,4096]{1,0:T(8,128)(2,1)} %bitcast.61, bf16[1,4096,384]{2,1,0:T(8,128)(2,1)} %param.10), kind=kOutput, calls=%fused_computation.8 | convolution fusion | flops 3221225472 | bytes 13107200 | tf_op jit(solution)/shard_map/dot_general | solution.py:70
  272.3 4.6 multiply_convert_fusion
  276.9 0.9 copy-done.2
  277.7 6.6 %convolution_convert_fusion = bf16[64,16,4096]{2,1,0:T(8,128)(2,1)} fusion(bf16[64,16,384]{2,1,0:T(8,128)(2,1)S(1)} %bitcast.63, bf16[1,384,4096]{2,1,0:T(8,128)(2,1)S(1)} %copy-done), kind=kOutput, calls=%fused_computation.4 | convolution fusion | flops 3225419776 | bytes 12320768 | tf_op jit(solution)/shard_map/dot_general | solution.py:73
  284.4 0.0 reduce-scatter.2.cloned.1.call-update
  284.4 0.0 copy-start.4
  284.4 0.0 copy-start.5
  284.4 78.8 %reduce-scatter.2.cloned.1.call-done = bf16[64,16,1024]{2,1,0:T(8,128)(2,1)} async-done(((bf16[64,16,4096]{2,1,0:T(8,128)(2,1)}), bf16[64,16,1024]{2,1,0:T(8,128)(2,1)}) %reduce-scatter.2.cloned.1.call-update) | async-done | bytes 2097168 | tf_op jit(solution)/shard_map/reduce_scatter | solution.py:74
  363.3 10.8 %all-to-all-start.2 = ((bf16[64,16,1024]{2,1,0:T(8,128)(2,1)}), bf16[64,16,1024]{2,1,0:T(8,128)(2,1)}, u32[]{:S(2)}, u32[]{:S(2)}) async-start(bf16[64,16,1024]{2,1,0:T(8,128)(2,1)} %reduce-scatter.2.cloned.1.call-done), calls=%async_computation.3 | async-start | bytes 4194304 | tf_op jit(solution)/shard_map/all_to_all | solution.py:80
  374.0 0.3 all-reduce.2.cloned.1.call-start
  374.3 2.2 convolution_convert_fusion.1
  376.5 0.0 all-reduce.2.cloned.1.call-update
  376.5 0.2 copy.27
  376.7 47.4 %all-reduce.2.cloned.1.call-done = bf16[1024,128]{1,0:T(8,128)(2,1)} async-done(((bf16[1024,128]{1,0:T(8,128)(2,1)}), bf16[1024,128]{1,0:T(8,128)(2,1)}) %all-reduce.2.cloned.1.call-update) | async-done | bytes 262160 | tf_op jit(solution)/shard_map/psum | solution.py:91
  424.1 1.3 fusion.20
  425.4 0.1 copy.26
  425.5 11.7 %cholesky.17 = f32[128,128]{1,0:T(8,128)S(1)} custom-call(f32[128,128]{1,0:T(8,128)S(1)} %fusion.13), custom_call_target="Cholesky" | custom-call | tf_op jit(solution)/shard_map/jit(cholesky)/cholesky | solution.py:92
  437.3 0.6 compare_reduce_fusion
  437.9 0.7 fusion.10
  438.6 9.8 %custom-call.7 = f32[1,128,128]{1,2,0:T(8,128)S(1)} custom-call(f32[1,128,128]{2,1,0:T(8,128)S(1)} %fusion.10), custom_call_target="InvertDiagBlocksLowerTriangular" | custom-call | tf_op jit(solution)/shard_map/jit(_solve_triangular)/triangular_solve | solution.py:96
  448.4 1.5 fusion.21
  449.9 1.0 convolution_bitcast_fusion
  451.0 0.0 all-to-all-done.2
  451.0 5.3 %gather_fusion.1 = bf16[512,1024]{1,0:T(8,128)(2,1)} fusion(bf16[1024,1024]{1,0:T(8,128)(2,1)} %bitcast.11, s32[1024]{0:T(1024)S(1)} %pad_clamp_fusion), kind=kCustom, calls=%fused_computation.1 | custom fusion | bytes 2099200 | tf_op jit(solution)/shard_map/gather | solution.py:81
  456.3 2.3 reshape.115
  458.6 1.9 fusion.19
  460.5 0.8 copy.32
  (19 shorter events, 0.2 us)
Async XLA Ops:
  7.2 270.6 %copy-start = (bf16[1,384,4096]{2,1,0:T(8,128)(2,1)S(1)}, bf16[1,384,4096]{2,1,0:T(8,128)(2,1)}, u32[]{:S(2)}) copy-start(bf16[1,384,4096]{2,1,0:T(8,128)(2,1)} %param.12) | copy-start | bytes 9437188
  7.2 33.5 %copy-start.3 = (bf16[128,1024]{1,0:T(8,128)(2,1)S(1)}, bf16[128,1024]{1,0:T(8,128)(2,1)}, u32[]{:S(2)}) copy-start(bf16[128,1024]{1,0:T(8,128)(2,1)} %param.7) | copy-start | bytes 786436
  7.2 21.6 %collective-permute-start = (bf16[128,1024]{1,0:T(8,128)(2,1)}, bf16[128,1024]{1,0:T(8,128)(2,1)}, u32[]{:S(2)}, u32[]{:S(2)}) collective-permute-start(bf16[128,1024]{1,0:T(8,128)(2,1)} %param.7), channel_id=1, source_target_pairs={{0,64},{64,128},{128,192},{192,0},{1,65},{65,129},{129,193},{193,1... | collective-permute-start | bytes 786440 | tf_op jit(solution)/shard_map/ppermute | solution.py:21
  8.8 32.0 %collective-permute-start.2 = (bf16[128,1024]{1,0:T(8,128)(2,1)}, bf16[128,1024]{1,0:T(8,128)(2,1)}, u32[]{:S(2)}, u32[]{:S(2)}) collective-permute-start(bf16[128,1024]{1,0:T(8,128)(2,1)} %param.7), channel_id=1, source_target_pairs={{0,192},{64,0},{128,64},{192,128},{1,193},{65,1},{129,65},{193,129... | collective-permute-start | bytes 786440 | tf_op jit(solution)/shard_map/ppermute | solution.py:23
  15.8 46.4 %all-to-all-start = ((bf16[64,1,1]{2,1,0:T(2,128)(2,1)}), bf16[64,1,1]{2,1,0:T(2,128)(2,1)S(1)}, u32[]{:S(2)}, u32[]{:S(2)}) async-start(bf16[64,1,1]{2,1,0:T(2,128)(2,1)} %copy.22), calls=%async_computation | async-start | bytes 65536 | tf_op jit(solution)/shard_map/all_to_all | solution.py:59
  28.8 10.0 %collective-permute-start.1 = (bf16[128,1024]{1,0:T(8,128)(2,1)}, bf16[128,1024]{1,0:T(8,128)(2,1)}, u32[]{:S(2)}, u32[]{:S(2)}) collective-permute-start(bf16[128,1024]{1,0:T(8,128)(2,1)} %collective-permute-done), channel_id=1, source_target_pairs={{0,64},{64,128},{128,192},{192,0},{1,65},{65,129},{129,193},{193,1... | collective-permute-start | bytes 786440 | tf_op jit(solution)/shard_map/ppermute | solution.py:21
  62.2 194.9 %all-to-all-start.1 = ((bf16[64,16,4096]{2,1,0:T(8,128)(2,1)}), bf16[64,16,4096]{2,1,0:T(8,128)(2,1)}, u32[]{:S(2)}, u32[]{:S(2)}) async-start(bf16[64,16,4096]{2,1,0:T(8,128)(2,1)} %bitcast.60), calls=%async_computation.1 | async-start | bytes 16777216 | tf_op jit(solution)/shard_map/all_to_all | solution.py:58
  72.7 290.6 %reduce-scatter.2.cloned.1.call-start = ((), (), s32[]{:S(2)}) async-start(), calls=%async_computation.4 | async-start | bytes 10485760 | tf_op jit(solution)/shard_map/reduce_scatter | solution.py:74
  264.3 8.0 %copy-start.1 = (bf16[64,16,4096]{2,1,0:T(8,128)(2,1)S(1)}, bf16[64,16,4096]{2,1,0:T(8,128)(2,1)}, u32[]{:S(2)}) copy-start(bf16[64,16,4096]{2,1,0:T(8,128)(2,1)} %broadcast_select_fusion) | copy-start | bytes 25165828
  264.3 8.0 %copy-start.6 = (bf16[1,4096,384]{2,1,0:T(8,128)(2,1)S(1)}, bf16[1,4096,384]{2,1,0:T(8,128)(2,1)}, u32[]{:S(2)}) copy-start(bf16[1,4096,384]{2,1,0:T(8,128)(2,1)} %param.11) | copy-start | bytes 9437188
  276.9 0.9 copy-start.2
  284.4 89.9 %copy-start.4 = (bf16[384,128]{1,0:T(8,128)(2,1)S(1)}, bf16[384,128]{1,0:T(8,128)(2,1)}, u32[]{:S(2)}) copy-start(bf16[384,128]{1,0:T(8,128)(2,1)} %param.13) | copy-start | bytes 294916
  284.4 92.1 %copy-start.5 = (f32[128,4]{0,1:T(4,128)S(1)}, f32[128,4]{0,1:T(4,128)}, u32[]{:S(2)}) copy-start(f32[128,4]{0,1:T(4,128)} %param.9) | copy-start | bytes 6148
  363.3 87.7 %all-to-all-start.2 = ((bf16[64,16,1024]{2,1,0:T(8,128)(2,1)}), bf16[64,16,1024]{2,1,0:T(8,128)(2,1)}, u32[]{:S(2)}, u32[]{:S(2)}) async-start(bf16[64,16,1024]{2,1,0:T(8,128)(2,1)} %reduce-scatter.2.cloned.1.call-done), calls=%async_computation.3 | async-start | bytes 4194304 | tf_op jit(solution)/shard_map/all_to_all | solution.py:80
  374.0 50.1 %all-reduce.2.cloned.1.call-start = ((), (), s32[]{:S(2)}) async-start(), calls=%async_computation.5 | async-start | bytes 524288 | tf_op jit(solution)/shard_map/psum | solution.py:91
Sparse Core Ops, SparseCore 0:
  284.5 78.6 reduce-scatter.1
  377.8 46.2 all-reduce.1
